TPU v7x, 32 devices: a whole 2x2x4 slice. The times are simulated.
32 devices in a mesh: lat: 4 (over z), lon: 8 (over y, x, core).
Axes of the slice: x: 2, y: 2, z: 4, core: 2. Of those that a mesh axis runs over, the one named last changes fastest.
Arguments:
- latents: bfloat16 [64, 128, 256], P('lat', 'lon'), may hold values from -6 to 6
- conv_weight: bfloat16 [9, 256, 256], replicated, may hold values from -0.125 to 0.125
- map_weight: bfloat16 [256, 1024], replicated, may hold values from -0.375 to 0.375
- map_bias: float32 [1024], replicated, may hold values from -6 to 6
- input_weight: float32 [3, 512], replicated, may hold values from -3.5 to 3.5
- hidden_weight: bfloat16 [1, 512, 512], replicated, may hold values from -0.25 to 0.25
- output_weight: float32 [512], replicated, may hold values from -0.25 to 0.25
- hit_owner: int32 [768], P(('lat', 'lon')), may hold values from 0 to 31, as said below
- serve_block: int32 [32, 32], P(('lat', 'lon')), may hold values from -1 to 1, as said below
- query_grid: int32 [3, 49152], P(None, ('lat', 'lon')), may hold values from 0 to 127, as said below
- cotangent: float32 [49152], P(('lat', 'lon')), may hold values from -6 to 6
Outputs:
- latent_grad: float32 [64, 128, 256], P('lat', 'lon')
- conv_grad: float32 [9, 256, 256], replicated
- map_grad: float32 [256, 1024], replicated
- map_bias_grad: float32 [1024], replicated
- input_grad: float32 [3, 512], replicated
- hidden_grad: float32 [1, 512, 512], replicated
- output_grad: float32 [512], replicated
Inputs may be any that keep to these rules, and one draw needn't show every extreme that they name: `hit_owner`: each device's 24 entries name distinct devices, numbered lat index times the size of lon plus lon index. `serve_block`: entry [o, r] is a block of device o, 0 to 1, when the list of device r names o, and -1 otherwise. `query_grid`: row 0 is the cell within the block (row-major over 8 rows of 16 cells), row 1 the sub-cell (0 to 35, row-major), row 2 the level (0 to 36).
All inputs are finite; a program needn't handle non-finite values.
Results may differ from a plain program's by a relative error of at most 0.0095.
Values may be sent and summed in bfloat16 or wider, within the bound.
No kernel may reach another device: no remote copies, remote signals or barrier semaphores. Data moves between devices by JAX's collectives and lax.ppermute only.
A program may use at most 128 MiB of HBM per device.

v0:
```python
import jax
import jax.numpy as jnp
from jax import lax
from jax.sharding import PartitionSpec as P

BLOCK = 128
LEVELS = 37
SUB = 6
OMEGA = 30.0


def padded_2(block, sides, width):
    for axis, dim in sides:
        count = lax.axis_size(axis)
        forward = [(i, i + 1) for i in range(count - 1)]
        forward.append((count - 1, 0))
        backward = [(target, source) for source, target in forward]
        low = lax.ppermute(
            lax.slice_in_dim(block, block.shape[dim] - width, None, axis=dim), axis, forward
        )
        high = lax.ppermute(lax.slice_in_dim(block, 0, width, axis=dim), axis, backward)
        block = jnp.concatenate([low, block, high], axis=dim)
    return block


def conv_apply(padded, kernel, row_count, col_count, flipped):
    channels = padded.shape[-1]
    result = jnp.zeros((row_count * col_count, kernel.shape[-1]), jnp.float32)
    for shift_a in (-1, 0, 1):
        for shift_b in (-1, 0, 1):
            tap_index = (shift_a + 1) * 3 + shift_b + 1
            if flipped:
                window = padded[
                    1 - shift_a : 1 - shift_a + row_count, 1 - shift_b : 1 - shift_b + col_count
                ]
                matrix = kernel[tap_index].T
            else:
                window = padded[
                    1 + shift_a : 1 + shift_a + row_count, 1 + shift_b : 1 + shift_b + col_count
                ]
                matrix = kernel[tap_index]
            result = result + jnp.dot(
                window.reshape(row_count * col_count, channels),
                matrix,
                preferred_element_type=jnp.float32,
            )
    return result


def conv_weight_grad(padded, grads, row_count, col_count):
    flat_grads = grads.reshape(row_count * col_count, -1)
    pieces = []
    for shift_a in (-1, 0, 1):
        for shift_b in (-1, 0, 1):
            window = padded[
                1 + shift_a : 1 + shift_a + row_count, 1 + shift_b : 1 + shift_b + col_count
            ]
            window = window.reshape(row_count * col_count, -1)
            pieces.append(jnp.dot(window.T, flat_grads, preferred_element_type=jnp.float32))
    return jnp.stack(pieces)


def close_poles(padded, lat_pos, lat_parts):
    top_rim = jnp.where(lat_pos == 0, jnp.zeros_like(padded[:1]), padded[:1])
    bottom_rim = jnp.where(lat_pos == lat_parts - 1, jnp.zeros_like(padded[-1:]), padded[-1:])
    return jnp.concatenate([top_rim, padded[1:-1], bottom_rim], axis=0)


def split_parts(values):
    upper = values.astype(jnp.bfloat16)
    lower = (values - upper.astype(jnp.float32)).astype(jnp.bfloat16)
    return (upper, lower)


def query_coords(
    cell_index, sub_index, level_index, lat_base, lon_base, lon_tile, lat_cells, lon_cells
):
    row_index = lat_base[:, None] + cell_index // lon_tile
    col_index = lon_base[:, None] + cell_index % lon_tile
    lat_coord = ((row_index * SUB + sub_index // SUB).astype(jnp.float32) + 0.5) / (
        lat_cells * SUB
    ) * 2.0 - 1.0
    lon_coord = ((col_index * SUB + sub_index % SUB).astype(jnp.float32) + 0.5) / (
        lon_cells * SUB
    ) * 2.0 - 1.0
    level_coord = (level_index.astype(jnp.float32) + 0.5) / LEVELS * 2.0 - 1.0
    return jnp.stack([lat_coord.reshape(-1), lon_coord.reshape(-1), level_coord.reshape(-1)])


def sine_grads(
    features, coords, cotan_rows, map_weight, map_bias, input_weight, hidden_weight, output_weight
):
    hidden_size = input_weight.shape[1]
    depth_count = map_weight.shape[1] // hidden_size
    shifts = jnp.dot(features, map_weight, preferred_element_type=jnp.float32) + map_bias
    linear = (
        coords[0][:, None] * input_weight[0]
        + coords[1][:, None] * input_weight[1]
        + coords[2][:, None] * input_weight[2]
    )
    preacts = [OMEGA * linear + shifts[:, :hidden_size]]
    layer_index = 1
    previous = jnp.sin(preacts[-1]).astype(jnp.bfloat16)
    inputs_rounded = [previous]
    preacts.append(
        jnp.dot(previous, hidden_weight[layer_index - 1], preferred_element_type=jnp.float32)
        + shifts[:, layer_index * hidden_size : (layer_index + 1) * hidden_size]
    )
    last_act = jnp.sin(preacts[-1])
    output_grad = jnp.dot(cotan_rows, last_act, precision=lax.Precision.HIGHEST)
    act_grad = cotan_rows[:, None] * output_weight[None, :]
    pre_grads = [None] * depth_count
    rounded_grads = [None] * depth_count
    hidden_grads = [None] * (depth_count - 1)
    for layer_index in range(depth_count - 1, -1, -1):
        pre_grads[layer_index] = act_grad * jnp.cos(preacts[layer_index])
        rounded_grads[layer_index] = pre_grads[layer_index].astype(jnp.bfloat16)
        if layer_index > 0:
            hidden_grads[layer_index - 1] = jnp.dot(
                inputs_rounded[layer_index - 1].T,
                rounded_grads[layer_index],
                preferred_element_type=jnp.float32,
            )
            act_grad = jnp.dot(
                rounded_grads[layer_index],
                hidden_weight[layer_index - 1].T,
                preferred_element_type=jnp.float32,
            )
    input_grad = OMEGA * jnp.dot(coords, pre_grads[0], precision=lax.Precision.HIGHEST)
    mod_grads = jnp.concatenate(rounded_grads, axis=1)
    bias_grad = jnp.sum(jnp.concatenate(pre_grads, axis=1), axis=0)
    map_grad = jnp.dot(features.T, mod_grads, preferred_element_type=jnp.float32)
    feature_grads = jnp.dot(mod_grads, map_weight.T, preferred_element_type=jnp.float32)
    return (feature_grads, (map_grad, bias_grad, input_grad, jnp.stack(hidden_grads), output_grad))


def run_groups(
    blocks,
    cell_index,
    sub_index,
    level_index,
    lat_base,
    lon_base,
    cotan_rows,
    weights,
    lon_tile,
    lat_cells,
    lon_cells,
):
    group_count = blocks.shape[0]
    block_rows = blocks.shape[1]
    channels = blocks.shape[2]
    step_size = 8
    turns = group_count // step_size

    def split_turns(source):
        return source.reshape((turns, step_size) + source.shape[1:])

    inputs = (
        split_turns(blocks),
        split_turns(cell_index),
        split_turns(sub_index),
        split_turns(level_index),
        split_turns(lat_base),
        split_turns(lon_base),
        split_turns(cotan_rows),
    )
    map_weight, map_bias, input_weight, hidden_weight, output_weight = weights
    initial = (
        jnp.zeros(map_weight.shape, jnp.float32),
        jnp.zeros(map_bias.shape, jnp.float32),
        jnp.zeros(input_weight.shape, jnp.float32),
        jnp.zeros(hidden_weight.shape, jnp.float32),
        jnp.zeros(output_weight.shape, jnp.float32),
    )

    def advance(grad_totals, slices):
        block_part, cell_part, sub_part, level_part, latb_part, lonb_part, cotan_part = slices
        onehot = (
            cell_part[:, :, None] == jnp.arange(block_rows, dtype=jnp.int32)[None, None, :]
        ).astype(jnp.bfloat16)
        features_q = jnp.einsum(
            "hgb,hbc->hgc", onehot, block_part, preferred_element_type=jnp.float32
        ).astype(jnp.bfloat16)
        coords = query_coords(
            cell_part, sub_part, level_part, latb_part, lonb_part, lon_tile, lat_cells, lon_cells
        )
        feature_grads, grads = sine_grads(
            features_q.reshape(-1, channels),
            coords,
            cotan_part.reshape(-1),
            map_weight,
            map_bias,
            input_weight,
            hidden_weight,
            output_weight,
        )
        upper, lower = split_parts(
            feature_grads.reshape(onehot.shape[0], onehot.shape[1], channels)
        )
        block_grads = jnp.einsum(
            "hgb,hgc->hbc", onehot, upper, preferred_element_type=jnp.float32
        ) + jnp.einsum("hgb,hgc->hbc", onehot, lower, preferred_element_type=jnp.float32)
        return (jax.tree.map(jnp.add, grad_totals, grads), block_grads)

    grad_totals, block_grads = lax.scan(advance, initial, inputs)
    return (block_grads.reshape(group_count, block_rows, channels), grad_totals)


def on_device(
    latents,
    conv_weight,
    map_weight,
    map_bias,
    input_weight,
    hidden_weight,
    output_weight,
    hit_owner,
    serve_block,
    query_grid,
    cotangent,
):
    lat_tile, lon_tile, channels = latents.shape
    lat_parts = lax.axis_size("lat")
    lon_parts = lax.axis_size("lon")
    dev_count = lat_parts * lon_parts
    lat_cells = lat_tile * lat_parts
    lon_cells = lon_tile * lon_parts
    block_rows = BLOCK
    tile_blocks = lat_tile * lon_tile // block_rows
    rows_per_block = block_rows // lon_tile
    lat_pos = lax.axis_index("lat")
    lon_pos = lax.axis_index("lon")
    padded = close_poles(padded_2(latents, (("lat", 0), ("lon", 1)), 1), lat_pos, lat_parts)
    features = conv_apply(padded, conv_weight, lat_tile, lon_tile, False).astype(jnp.bfloat16)
    own_blocks = features.reshape(tile_blocks, block_rows * channels)
    serve_row = serve_block[0]
    selector = (serve_row[:, None] == jnp.arange(tile_blocks, dtype=jnp.int32)[None, :]).astype(
        jnp.bfloat16
    )
    slot_blocks = jnp.dot(selector, own_blocks, preferred_element_type=jnp.float32).astype(
        jnp.bfloat16
    )
    slot_blocks = slot_blocks.reshape(dev_count, block_rows, channels)
    weights = (map_weight, map_bias, input_weight, hidden_weight, output_weight)
    hit_count = hit_owner.shape[0]
    group_size = cotangent.shape[0] // hit_count
    grid_groups = query_grid.reshape(3, hit_count, group_size).transpose(1, 0, 2)
    grid_slots = jnp.zeros((dev_count, 3, group_size), jnp.int32).at[hit_owner].set(grid_groups)
    cotan_slots = (
        jnp.zeros((dev_count, group_size), jnp.float32)
        .at[hit_owner]
        .set(cotangent.reshape(hit_count, group_size))
    )
    grid_in, cotan_in = (
        lax.all_to_all(grid_slots, ("lat", "lon"), split_axis=0, concat_axis=0, tiled=True),
        lax.all_to_all(cotan_slots, ("lat", "lon"), split_axis=0, concat_axis=0, tiled=True),
    )
    lat_base = lat_pos * lat_tile + serve_row * rows_per_block
    lon_base = jnp.zeros((dev_count,), jnp.int32) + lon_pos * lon_tile
    slot_grads, grad_totals = run_groups(
        slot_blocks,
        grid_in[:, 0],
        grid_in[:, 1],
        grid_in[:, 2],
        lat_base,
        lon_base,
        cotan_in,
        weights,
        lon_tile,
        lat_cells,
        lon_cells,
    )
    slot_upper, slot_lower = split_parts(slot_grads.reshape(dev_count, block_rows * channels))
    tile_grads = jnp.dot(selector.T, slot_upper, preferred_element_type=jnp.float32) + jnp.dot(
        selector.T, slot_lower, preferred_element_type=jnp.float32
    )
    feature_grad = tile_grads.reshape(lat_tile, lon_tile, channels).astype(jnp.bfloat16)
    padded_grad = close_poles(
        padded_2(feature_grad, (("lat", 0), ("lon", 1)), 1), lat_pos, lat_parts
    )
    latent_grad = conv_apply(padded_grad, conv_weight, lat_tile, lon_tile, True).reshape(
        lat_tile, lon_tile, channels
    )
    conv_local = conv_weight_grad(padded, feature_grad, lat_tile, lon_tile)
    totals = lax.psum(
        (
            conv_local,
            grad_totals[0],
            grad_totals[1],
            grad_totals[2],
            grad_totals[3],
            grad_totals[4],
        ),
        ("lat", "lon"),
    )
    grad_scale = float(hit_count * group_size * dev_count) ** (-0.5)
    return (
        latent_grad,
        totals[0] * grad_scale,
        totals[1] * grad_scale,
        totals[2] * grad_scale,
        totals[3] * grad_scale,
        totals[4] * grad_scale,
        totals[5] * grad_scale,
    )


def solution(mesh):
    placed = (
        P("lat", "lon", None),
        P(),
        P(),
        P(),
        P(),
        P(),
        P(),
        P(("lat", "lon")),
        P(("lat", "lon"), None),
        P(None, ("lat", "lon")),
        P(("lat", "lon")),
    )
    return jax.shard_map(
        on_device,
        mesh=mesh,
        in_specs=placed,
        out_specs=(P("lat", "lon", None), P(), P(), P(), P(), P(), P()),
        check_vma=False,
    )
```

profile of v0, /device:TPU:0, one launch (start us, length us, event | category | flops | bytes accessed | tf_op | source)
XLA Modules:
  0.0 379.6 jit_solution(5831723974505579724)
XLA Ops:
  8.0 5.1 %collective-permute-start.1 = (bf16[1,16,256]{2,1,0:T(8,128)(2,1)S(1)}, bf16[1,16,256]{2,1,0:T(8,128)(2,1)S(1)}, u32[]{:S(2)}, u32[]{:S(2)}) collective-permute-start(bf16[1,16,256]{2,1,0:T(8,128)(2,1)S(1)} %get-tuple-element.522), channel_id=1, source_target_pairs={{8,0},{16,8},{24,16},{0,24},{9,1},{17,9},{25,17},{1,25},{10,2},{18... | collective-permute-start | bytes 24584 | tf_op jit(solution)/shard_map/ppermute | solution.py:21
  16.9 6.2 %all-to-all-start = ((s32[32,1,192]{2,1,0:T(1,128)}), s32[32,1,192]{2,1,0:T(1,128)}, u32[]{:S(2)}, u32[]{:S(2)}) async-start(s32[32,1,192]{2,1,0:T(1,128)} %reshape.659), calls=%async_computation | async-start | bytes 65536 | tf_op jit(solution)/shard_map/all_to_all | solution.py:256
  34.9 4.9 %all-to-all-start.1 = ((f32[32,1,64]{2,1,0:T(1,128)}), f32[32,1,64]{2,1,0:T(1,128)S(1)}, u32[]{:S(2)}, u32[]{:S(2)}) async-start(f32[32,1,64]{2,1,0:T(1,128)} %bitcast.22), calls=%async_computation.1 | async-start | bytes 32768 | tf_op jit(solution)/shard_map/all_to_all | solution.py:257
  42.0 5.0 %all-to-all-done.1 = f32[32,1,64]{2,1,0:T(1,128)S(1)} async-done(((f32[32,1,64]{2,1,0:T(1,128)}), f32[32,1,64]{2,1,0:T(1,128)S(1)}, u32[]{:S(2)}, u32[]{:S(2)}) %all-to-all-start.1) | async-done | bytes 8224 | tf_op jit(solution)/shard_map/all_to_all | solution.py:257
  47.0 110.0 %while.24 = (s32[]{:T(128)}, f32[256,1024]{1,0:T(8,128)S(1)}, f32[1024]{0:T(1024)S(1)}, f32[3,512]{1,0:T(4,128)}, f32[1,512,512]{2,1,0:T(8,128)}, /*index=5*/f32...) while((s32[]{:T(128)}, f32[256,1024]{1,0:T(8,128)S(1)}, ...), condition=%wide.region_4.5_spmd.clone, body=%wide.region_2.4_spmd.clone.sunk | while | flops 1739577856 | bytes 41995484 | solution.py:206
  51.5 7.2 %fusion.204 = (bf16[512,512]{1,0:T(8,128)(2,1)S(1)}, f32[512,512]{1,0:T(8,128)S(1)}, f32[512,512]{1,0:T(8,128)S(1)}) fusion(f32[512]{0:T(512)S(1)} %copy-done.28, f32[512]{0:T(512)S(1)} %mul.582, f32[512,1024]{1,0:T(8,128)S(1)} %convolution_add_fusion.19, bf16[1,512,512]{2,1,0:T(8,128)(2,1)S(1)} %copy-done.27, f32[512]{0:T(512)S(1)} %bitcast.281, ...), kind=kOutput, calls=%fused_computation.233.clone.1 | convolution fusion | flops 271581184 | bytes 5259264 | tf_op jit(solution)/shard_map/while/body/eval_jaxpr/dot_general | solution.py:106
  58.6 4.0 %fusion.208 = f32[1,512]{1,0:T(1,128)S(1)} fusion(f32[512,1]{0,1:T(1,128)S(1)} %reshape.662, f32[512,512]{1,0:T(8,128)S(1)} %get-tuple-element.679), kind=kOutput, calls=%fused_computation.17.clone.1 | convolution fusion | flops 3145728 | bytes 1052672 | tf_op jit(solution)/shard_map/while/body/eval_jaxpr/dot_general | solution.py:110
  62.7 4.1 %fusion.207 = f32[1,512,512]{2,1,0:T(8,128)S(1)} fusion(bf16[512,512]{1,0:T(8,128)(2,1)S(1)} %get-tuple-element.673, f32[1,512,512]{2,1,0:T(8,128)S(1)} %copy-done.4, pred[]{:T(512)S(6)} %compare.35, f32[512,1024]{1,0:T(8,128)S(1)} %convolution_add_fusion.19, f32[512]{0:T(512)S(1)} %bitcast.282, f32[512]{0:T(512)S(1)} %sub.107, ...), kind=kOutput, calls=%fused_computation.11.clone.1 | convolution fusion | flops 271056896 | bytes 3682305 | tf_op jit(solution)/shard_map/while/body/eval_jaxpr/dot_general | solution.py:119
  66.8 3.8 %fusion.205 = (bf16[512,512]{1,0:T(8,128)(2,1)S(1)}, f32[512,512]{1,0:T(8,128)S(1)}) fusion(f32[512,1024]{1,0:T(8,128)S(1)} %convolution_add_fusion.19, f32[512]{0:T(512)S(1)} %bitcast.283, f32[512]{0:T(512)S(1)} %sub.107, f32[512]{0:T(512)S(1)} %bitcast.286, f32[512]{0:T(512)S(1)} %get-tuple-element.670, f32[512]{0:T(512)S(1)} %bitcast.280, ...), kind=kOutput, calls=%fused_computation.235.clone.1 | convolution fusion | flops 270794752 | bytes 3682304 | tf_op jit(solution)/shard_map/while/body/eval_jaxpr/dot_general | solution.py:124
  79.0 7.2 %fusion.204 = (bf16[512,512]{1,0:T(8,128)(2,1)S(1)}, f32[512,512]{1,0:T(8,128)S(1)}, f32[512,512]{1,0:T(8,128)S(1)}) fusion(f32[512]{0:T(512)S(1)} %copy-done.28, f32[512]{0:T(512)S(1)} %mul.582, f32[512,1024]{1,0:T(8,128)S(1)} %convolution_add_fusion.19, bf16[1,512,512]{2,1,0:T(8,128)(2,1)S(1)} %copy-done.27, f32[512]{0:T(512)S(1)} %bitcast.281, ...), kind=kOutput, calls=%fused_computation.233.clone.1 | convolution fusion | flops 271581184 | bytes 5259264 | tf_op jit(solution)/shard_map/while/body/eval_jaxpr/dot_general | solution.py:106
  86.2 4.0 %fusion.208 = f32[1,512]{1,0:T(1,128)S(1)} fusion(f32[512,1]{0,1:T(1,128)S(1)} %reshape.662, f32[512,512]{1,0:T(8,128)S(1)} %get-tuple-element.679), kind=kOutput, calls=%fused_computation.17.clone.1 | convolution fusion | flops 3145728 | bytes 1052672 | tf_op jit(solution)/shard_map/while/body/eval_jaxpr/dot_general | solution.py:110
  90.2 4.1 %fusion.207 = f32[1,512,512]{2,1,0:T(8,128)S(1)} fusion(bf16[512,512]{1,0:T(8,128)(2,1)S(1)} %get-tuple-element.673, f32[1,512,512]{2,1,0:T(8,128)S(1)} %copy-done.4, pred[]{:T(512)S(6)} %compare.35, f32[512,1024]{1,0:T(8,128)S(1)} %convolution_add_fusion.19, f32[512]{0:T(512)S(1)} %bitcast.282, f32[512]{0:T(512)S(1)} %sub.107, ...), kind=kOutput, calls=%fused_computation.11.clone.1 | convolution fusion | flops 271056896 | bytes 3682305 | tf_op jit(solution)/shard_map/while/body/eval_jaxpr/dot_general | solution.py:119
  94.3 3.8 %fusion.205 = (bf16[512,512]{1,0:T(8,128)(2,1)S(1)}, f32[512,512]{1,0:T(8,128)S(1)}) fusion(f32[512,1024]{1,0:T(8,128)S(1)} %convolution_add_fusion.19, f32[512]{0:T(512)S(1)} %bitcast.283, f32[512]{0:T(512)S(1)} %sub.107, f32[512]{0:T(512)S(1)} %bitcast.286, f32[512]{0:T(512)S(1)} %get-tuple-element.670, f32[512]{0:T(512)S(1)} %bitcast.280, ...), kind=kOutput, calls=%fused_computation.235.clone.1 | convolution fusion | flops 270794752 | bytes 3682304 | tf_op jit(solution)/shard_map/while/body/eval_jaxpr/dot_general | solution.py:124
  106.5 7.2 %fusion.204 = (bf16[512,512]{1,0:T(8,128)(2,1)S(1)}, f32[512,512]{1,0:T(8,128)S(1)}, f32[512,512]{1,0:T(8,128)S(1)}) fusion(f32[512]{0:T(512)S(1)} %copy-done.28, f32[512]{0:T(512)S(1)} %mul.582, f32[512,1024]{1,0:T(8,128)S(1)} %convolution_add_fusion.19, bf16[1,512,512]{2,1,0:T(8,128)(2,1)S(1)} %copy-done.27, f32[512]{0:T(512)S(1)} %bitcast.281, ...), kind=kOutput, calls=%fused_computation.233.clone.1 | convolution fusion | flops 271581184 | bytes 5259264 | tf_op jit(solution)/shard_map/while/body/eval_jaxpr/dot_general | solution.py:106
  113.7 4.0 %fusion.208 = f32[1,512]{1,0:T(1,128)S(1)} fusion(f32[512,1]{0,1:T(1,128)S(1)} %reshape.662, f32[512,512]{1,0:T(8,128)S(1)} %get-tuple-element.679), kind=kOutput, calls=%fused_computation.17.clone.1 | convolution fusion | flops 3145728 | bytes 1052672 | tf_op jit(solution)/shard_map/while/body/eval_jaxpr/dot_general | solution.py:110
  117.7 4.1 %fusion.207 = f32[1,512,512]{2,1,0:T(8,128)S(1)} fusion(bf16[512,512]{1,0:T(8,128)(2,1)S(1)} %get-tuple-element.673, f32[1,512,512]{2,1,0:T(8,128)S(1)} %copy-done.4, pred[]{:T(512)S(6)} %compare.35, f32[512,1024]{1,0:T(8,128)S(1)} %convolution_add_fusion.19, f32[512]{0:T(512)S(1)} %bitcast.282, f32[512]{0:T(512)S(1)} %sub.107, ...), kind=kOutput, calls=%fused_computation.11.clone.1 | convolution fusion | flops 271056896 | bytes 3682305 | tf_op jit(solution)/shard_map/while/body/eval_jaxpr/dot_general | solution.py:119
  121.8 3.8 %fusion.205 = (bf16[512,512]{1,0:T(8,128)(2,1)S(1)}, f32[512,512]{1,0:T(8,128)S(1)}) fusion(f32[512,1024]{1,0:T(8,128)S(1)} %convolution_add_fusion.19, f32[512]{0:T(512)S(1)} %bitcast.283, f32[512]{0:T(512)S(1)} %sub.107, f32[512]{0:T(512)S(1)} %bitcast.286, f32[512]{0:T(512)S(1)} %get-tuple-element.670, f32[512]{0:T(512)S(1)} %bitcast.280, ...), kind=kOutput, calls=%fused_computation.235.clone.1 | convolution fusion | flops 270794752 | bytes 3682304 | tf_op jit(solution)/shard_map/while/body/eval_jaxpr/dot_general | solution.py:124
  134.0 7.2 %fusion.204 = (bf16[512,512]{1,0:T(8,128)(2,1)S(1)}, f32[512,512]{1,0:T(8,128)S(1)}, f32[512,512]{1,0:T(8,128)S(1)}) fusion(f32[512]{0:T(512)S(1)} %copy-done.28, f32[512]{0:T(512)S(1)} %mul.582, f32[512,1024]{1,0:T(8,128)S(1)} %convolution_add_fusion.19, bf16[1,512,512]{2,1,0:T(8,128)(2,1)S(1)} %copy-done.27, f32[512]{0:T(512)S(1)} %bitcast.281, ...), kind=kOutput, calls=%fused_computation.233.clone.1 | convolution fusion | flops 271581184 | bytes 5259264 | tf_op jit(solution)/shard_map/while/body/eval_jaxpr/dot_general | solution.py:106
  141.1 4.0 %fusion.208 = f32[1,512]{1,0:T(1,128)S(1)} fusion(f32[512,1]{0,1:T(1,128)S(1)} %reshape.662, f32[512,512]{1,0:T(8,128)S(1)} %get-tuple-element.679), kind=kOutput, calls=%fused_computation.17.clone.1 | convolution fusion | flops 3145728 | bytes 1052672 | tf_op jit(solution)/shard_map/while/body/eval_jaxpr/dot_general | solution.py:110
  145.2 4.1 %fusion.207 = f32[1,512,512]{2,1,0:T(8,128)S(1)} fusion(bf16[512,512]{1,0:T(8,128)(2,1)S(1)} %get-tuple-element.673, f32[1,512,512]{2,1,0:T(8,128)S(1)} %copy-done.4, pred[]{:T(512)S(6)} %compare.35, f32[512,1024]{1,0:T(8,128)S(1)} %convolution_add_fusion.19, f32[512]{0:T(512)S(1)} %bitcast.282, f32[512]{0:T(512)S(1)} %sub.107, ...), kind=kOutput, calls=%fused_computation.11.clone.1 | convolution fusion | flops 271056896 | bytes 3682305 | tf_op jit(solution)/shard_map/while/body/eval_jaxpr/dot_general | solution.py:119
  149.3 3.8 %fusion.205 = (bf16[512,512]{1,0:T(8,128)(2,1)S(1)}, f32[512,512]{1,0:T(8,128)S(1)}) fusion(f32[512,1024]{1,0:T(8,128)S(1)} %convolution_add_fusion.19, f32[512]{0:T(512)S(1)} %bitcast.283, f32[512]{0:T(512)S(1)} %sub.107, f32[512]{0:T(512)S(1)} %bitcast.286, f32[512]{0:T(512)S(1)} %get-tuple-element.670, f32[512]{0:T(512)S(1)} %bitcast.280, ...), kind=kOutput, calls=%fused_computation.235.clone.1 | convolution fusion | flops 270794752 | bytes 3682304 | tf_op jit(solution)/shard_map/while/body/eval_jaxpr/dot_general | solution.py:124
  157.0 5.0 %copy.33 = f32[4,8,128,256]{3,1,2,0:T(8,128)S(1)} copy(f32[4,8,128,256]{3,2,1,0:T(8,128)} %get-tuple-element.323) | data formatting | bytes 8388608
  164.4 38.4 %all-reduce = (f32[1024]{0:T(1024)S(1)}, f32[3,512]{1,0:T(4,128)S(1)}, f32[512]{0:T(512)S(1)}) all-reduce(f32[1024]{0:T(1024)S(1)} %get-tuple-element.325, f32[3,512]{1,0:T(4,128)S(1)} %copy-done.18, f32[512]{0:T(512)S(1)} %copy-done.22), channel_id=1, replica_groups=mesh['lat'=4,'lon'=8] {'lat','lon'}, use_global_device_ids=true, to_apply=%region_7.8 | all-reduce | flops 3072 | bytes 24576 | tf_op jit(solution)/shard_map/psum | solution.py:286
  224.0 142.8 %all-reduce.4.cloned.1.call-done = (f32[9,256,256]{2,1,0:T(8,128)}, f32[256,1024]{1,0:T(8,128)}, f32[1,512,512]{2,1,0:T(8,128)}) async-done(((f32[9,256,256]{2,1,0:T(8,128)}, f32[256,1024]{1,0:T(8,128)}, f32[1,512,512]{2,1,0:T(8,128)}), (f32[9,256,256]{2,1,0:T(8,128)}, f32[256,1024]{1,0:T(8,128)}, f32[1,512,512]{2,1,0:T(8,128)})) %all-reduce.4.cloned.1.call-update) | async-done | bytes 4456464 | tf_op jit(solution)/shard_map/psum | solution.py:286
  (366 shorter events, 80.9 us)
Async XLA Ops:
  7.2 23.9 %copy-start.2 = (bf16[9,256,256]{2,1,0:T(8,128)(2,1)S(1)}, bf16[9,256,256]{2,1,0:T(8,128)(2,1)}, u32[]{:S(2)}) copy-start(bf16[9,256,256]{2,1,0:T(8,128)(2,1)} %param.14) | copy-start | bytes 3538948
  8.0 17.2 %collective-permute-start.1 = (bf16[1,16,256]{2,1,0:T(8,128)(2,1)S(1)}, bf16[1,16,256]{2,1,0:T(8,128)(2,1)S(1)}, u32[]{:S(2)}, u32[]{:S(2)}) collective-permute-start(bf16[1,16,256]{2,1,0:T(8,128)(2,1)S(1)} %get-tuple-element.522), channel_id=1, source_target_pairs={{8,0},{16,8},{24,16},{0,24},{9,1},{17,9},{25,17},{1,25},{10,2},{18... | collective-permute-start | bytes 24584 | tf_op jit(solution)/shard_map/ppermute | solution.py:21
  13.1 11.2 %collective-permute-start = (bf16[1,16,256]{2,1,0:T(8,128)(2,1)S(1)}, bf16[1,16,256]{2,1,0:T(8,128)(2,1)S(1)}, u32[]{:S(2)}, u32[]{:S(2)}) collective-permute-start(bf16[1,16,256]{2,1,0:T(8,128)(2,1)S(1)} %get-tuple-element.523), channel_id=1, source_target_pairs={{0,8},{8,16},{16,24},{24,0},{1,9},{9,17},{17,25},{25,1},{2,10},{10... | collective-permute-start | bytes 24584 | tf_op jit(solution)/shard_map/ppermute | solution.py:18
  16.9 18.1 %all-to-all-start = ((s32[32,1,192]{2,1,0:T(1,128)}), s32[32,1,192]{2,1,0:T(1,128)}, u32[]{:S(2)}, u32[]{:S(2)}) async-start(s32[32,1,192]{2,1,0:T(1,128)} %reshape.659), calls=%async_computation | async-start | bytes 65536 | tf_op jit(solution)/shard_map/all_to_all | solution.py:256
  25.2 5.5 %collective-permute-start.2 = (bf16[18,1,256]{2,1,0:T(2,128)(2,1)S(1)}, bf16[18,1,256]{2,1,0:T(2,128)(2,1)S(1)}, u32[]{:S(2)}, u32[]{:S(2)}) collective-permute-start(bf16[18,1,256]{2,1,0:T(2,128)(2,1)S(1)} %get-tuple-element.518), channel_id=1, source_target_pairs={{0,1},{1,2},{2,3},{3,4},{4,5},{5,6},{6,7},{7,0},{8,9},{9,10},{10,1... | collective-permute-start | bytes 27656 | tf_op jit(solution)/shard_map/ppermute | solution.py:18
  25.5 5.3 %collective-permute-start.3 = (bf16[18,1,256]{2,1,0:T(2,128)(2,1)S(1)}, bf16[18,1,256]{2,1,0:T(2,128)(2,1)S(1)}, u32[]{:S(2)}, u32[]{:S(2)}) collective-permute-start(bf16[18,1,256]{2,1,0:T(2,128)(2,1)S(1)} %get-tuple-element.519), channel_id=1, source_target_pairs={{1,0},{2,1},{3,2},{4,3},{5,4},{6,5},{7,6},{0,7},{9,8},{10,9},{11,1... | collective-permute-start | bytes 27656 | tf_op jit(solution)/shard_map/ppermute | solution.py:21
  32.4 14.6 %copy-start.1 = (bf16[256,1024]{1,0:T(8,128)(2,1)S(1)}, bf16[256,1024]{1,0:T(8,128)(2,1)}, u32[]{:S(2)}) copy-start(bf16[256,1024]{1,0:T(8,128)(2,1)} %param.15) | copy-start | bytes 1572868
  34.9 12.0 %all-to-all-start.1 = ((f32[32,1,64]{2,1,0:T(1,128)}), f32[32,1,64]{2,1,0:T(1,128)S(1)}, u32[]{:S(2)}, u32[]{:S(2)}) async-start(f32[32,1,64]{2,1,0:T(1,128)} %bitcast.22), calls=%async_computation.1 | async-start | bytes 32768 | tf_op jit(solution)/shard_map/all_to_all | solution.py:257
  39.8 327.0 %all-reduce.4.cloned.1.call-start = ((), (), s32[]{:S(2)}) async-start(), calls=%async_computation.2 | async-start | bytes 8912896 | tf_op jit(solution)/shard_map/psum | solution.py:286
  51.4 11.1 %copy-start.20 = (f32[512]{0:T(512)S(1)}, f32[512]{0:T(512)}, u32[]{:S(2)}) copy-start(f32[512]{0:T(512)} %get-tuple-element.706) | copy-start | bytes 6148 | tf_op jit(solution)/shard_map/while
  51.4 11.2 %copy-start.4 = (f32[1,512,512]{2,1,0:T(8,128)S(1)}, f32[1,512,512]{2,1,0:T(8,128)}, u32[]{:S(2)}) copy-start(f32[1,512,512]{2,1,0:T(8,128)} %get-tuple-element.705) | copy-start | bytes 3145732 | tf_op jit(solution)/shard_map/while
  79.0 11.1 %copy-start.20 = (f32[512]{0:T(512)S(1)}, f32[512]{0:T(512)}, u32[]{:S(2)}) copy-start(f32[512]{0:T(512)} %get-tuple-element.706) | copy-start | bytes 6148 | tf_op jit(solution)/shard_map/while
  79.0 11.2 %copy-start.4 = (f32[1,512,512]{2,1,0:T(8,128)S(1)}, f32[1,512,512]{2,1,0:T(8,128)}, u32[]{:S(2)}) copy-start(f32[1,512,512]{2,1,0:T(8,128)} %get-tuple-element.705) | copy-start | bytes 3145732 | tf_op jit(solution)/shard_map/while
  106.5 11.1 %copy-start.20 = (f32[512]{0:T(512)S(1)}, f32[512]{0:T(512)}, u32[]{:S(2)}) copy-start(f32[512]{0:T(512)} %get-tuple-element.706) | copy-start | bytes 6148 | tf_op jit(solution)/shard_map/while
  106.5 11.2 %copy-start.4 = (f32[1,512,512]{2,1,0:T(8,128)S(1)}, f32[1,512,512]{2,1,0:T(8,128)}, u32[]{:S(2)}) copy-start(f32[1,512,512]{2,1,0:T(8,128)} %get-tuple-element.705) | copy-start | bytes 3145732 | tf_op jit(solution)/shard_map/while
  134.0 11.1 %copy-start.20 = (f32[512]{0:T(512)S(1)}, f32[512]{0:T(512)}, u32[]{:S(2)}) copy-start(f32[512]{0:T(512)} %get-tuple-element.706) | copy-start | bytes 6148 | tf_op jit(solution)/shard_map/while
  134.0 11.2 %copy-start.4 = (f32[1,512,512]{2,1,0:T(8,128)S(1)}, f32[1,512,512]{2,1,0:T(8,128)}, u32[]{:S(2)}) copy-start(f32[1,512,512]{2,1,0:T(8,128)} %get-tuple-element.705) | copy-start | bytes 3145732 | tf_op jit(solution)/shard_map/while
  157.0 5.0 %copy-start = (f32[256,1024]{1,0:T(8,128)}, f32[256,1024]{1,0:T(8,128)S(1)}, u32[]{:S(2)}) copy-start(f32[256,1024]{1,0:T(8,128)S(1)} %get-tuple-element.324) | copy-start | bytes 3145732
  157.0 5.0 %copy-start.26 = (s32[1,32]{1,0:T(1,128)S(1)}, s32[1,32]{1,0:T(1,128)}, u32[]{:S(2)}) copy-start(s32[1,32]{1,0:T(1,128)} %param.21) | copy-start | bytes 388
  163.1 42.0 %copy-start.9 = (bf16[16,16,256]{2,1,0:T(8,128)(2,1)S(1)}, bf16[16,16,256]{2,1,0:T(8,128)(2,1)}, u32[]{:S(2)}) copy-start(bf16[16,16,256]{2,1,0:T(8,128)(2,1)} %copy-done.8) | copy-start | bytes 393220
  203.4 12.1 %collective-permute-start.4 = (bf16[1,16,256]{2,1,0:T(8,128)(2,1)S(1)}, bf16[1,16,256]{2,1,0:T(8,128)(2,1)S(1)}, u32[]{:S(2)}, u32[]{:S(2)}) collective-permute-start(bf16[1,16,256]{2,1,0:T(8,128)(2,1)S(1)} %get-tuple-element.521), channel_id=1, source_target_pairs={{0,8},{8,16},{16,24},{24,0},{1,9},{9,17},{17,25},{25,1},{2,10},{10... | collective-permute-start | bytes 24584 | tf_op jit(solution)/shard_map/ppermute | solution.py:18
  213.2 3.7 collective-permute-start.5
  216.9 4.1 %collective-permute-start.6 = (bf16[18,1,256]{2,1,0:T(2,128)(2,1)S(1)}, bf16[18,1,256]{2,1,0:T(2,128)(2,1)S(1)}, u32[]{:S(2)}, u32[]{:S(2)}) collective-permute-start(bf16[18,1,256]{2,1,0:T(2,128)(2,1)S(1)} %get-tuple-element.514), channel_id=1, source_target_pairs={{0,1},{1,2},{2,3},{3,4},{4,5},{5,6},{6,7},{7,0},{8,9},{9,10},{10,1... | collective-permute-start | bytes 27656 | tf_op jit(solution)/shard_map/ppermute | solution.py:18
  217.0 4.1 %collective-permute-start.7 = (bf16[18,1,256]{2,1,0:T(2,128)(2,1)S(1)}, bf16[18,1,256]{2,1,0:T(2,128)(2,1)S(1)}, u32[]{:S(2)}, u32[]{:S(2)}) collective-permute-start(bf16[18,1,256]{2,1,0:T(2,128)(2,1)S(1)} %get-tuple-element.515), channel_id=1, source_target_pairs={{1,0},{2,1},{3,2},{4,3},{5,4},{6,5},{7,6},{0,7},{9,8},{10,9},{11,1... | collective-permute-start | bytes 27656 | tf_op jit(solution)/shard_map/ppermute | solution.py:21
  (49 other events, 112.5 us)
Sparse Core Ops, SparseCore 0:
  220.4 146.3 all-reduce.3
where the time goes:
time: 381 us; the launch traced here: 380 us
  waiting for transfers between devices  150 us (39%)
  matrix products  110 us (29%)
  blocking collectives  38.4 us (10%)
  local copies, waits for them, and re-layouts  28.1 us (7%)
  starting transfers between devices  25.4 us (7%)
  between operations  14.6 us (4%)
  other arithmetic  12 us (3%)
    psum x1, waiting for transfers between devices, on_device(): lax.psum((conv_local, grad_totals[0], grad_totals[1], grad_totals[2], gra...  143 us
    psum x1, blocking collectives, on_device(): lax.psum((conv_local, grad_totals[0], grad_totals[1], grad_totals[2], gra...  38.4 us
    dot_general x4, matrix products, sine_grads(): jnp.dot(previous, hidden_weight[layer_index - 1], preferred_element_type=...  28.7 us
    dot_general x4, matrix products, sine_grads(): jnp.dot(inputs_rounded[layer_index - 1].T, rounded_grads[layer_index], pr...  16.2 us
    dot_general x4, matrix products, sine_grads(): output_grad = jnp.dot(cotan_rows, last_act, precision=lax.Precision.HIGHEST)  15.8 us
    dot_general x4, matrix products, sine_grads(): jnp.dot(rounded_grads[layer_index], hidden_weight[layer_index - 1].T, pre...  15.3 us
    ppermute x4, starting transfers between devices, padded_2(): lax.ppermute(lax.slice_in_dim(block, 0, width, axis=dim), axis, backward)  12.5 us
    dot_general x9, matrix products, conv_weight_grad(): jnp.dot(window.T, flat_grads, preferred_element_type=jnp.float32)  8.39 us
  transfers between devices with their start and end apart: 11, of which 4 were waited for; matrix products, arithmetic and copies ran while one was open for 7% of the time, Pallas kernels for 0%

commit v1 on v0

--- a/solution.py
+++ b/solution.py
@@ -283,17 +283,15 @@
         lat_tile, lon_tile, channels
     )
     conv_local = conv_weight_grad(padded, feature_grad, lat_tile, lon_tile)
-    totals = lax.psum(
-        (
-            conv_local,
-            grad_totals[0],
-            grad_totals[1],
-            grad_totals[2],
-            grad_totals[3],
-            grad_totals[4],
-        ),
-        ("lat", "lon"),
-    )
+    content = (
+        conv_local,
+        grad_totals[0],
+        grad_totals[1],
+        grad_totals[2],
+        grad_totals[3],
+        grad_totals[4],
+    )
+    totals = lax.psum(lax.psum(content, "lon"), "lat")
     grad_scale = float(hit_count * group_size * dev_count) ** (-0.5)
     return (
         latent_grad,

time: 381 us -> 435 us (1.14)
  waiting for transfers between devices: 150 us -> 199 us
  blocking collectives: 38.4 us -> 44.1 us
    psum x1 -> x2, waiting for transfers between devices: 143 us -> 189 us  [on_device(): totals = lax.psum(lax.psum(content, 'lon'), 'lat')]
    psum x1 -> x2, blocking collectives: 38.4 us -> 44.1 us  [on_device(): totals = lax.psum(lax.psum(content, 'lon'), 'lat')]
  transfers between devices with their start and end apart: 11 -> 12, of which waited for: 4 -> 5; matrix products, arithmetic and copies ran while one was open for 7% -> 5% of each run, Pallas kernels for 0% -> 0%
where the time goes in v1:
time: 435 us; the launch traced here: 434 us
  waiting for transfers between devices  199 us (46%)
  matrix products  111 us (26%)
  blocking collectives  44.1 us (10%)
  local copies, waits for them, and re-layouts  28.6 us (7%)
  starting transfers between devices  23.1 us (5%)
  between operations  14.6 us (3%)
  other arithmetic  12.8 us (3%)
    psum x2, waiting for transfers between devices, on_device(): totals = lax.psum(lax.psum(content, 'lon'), 'lat')  189 us
    psum x2, blocking collectives, on_device(): totals = lax.psum(lax.psum(content, 'lon'), 'lat')  44.1 us
    dot_general x4, matrix products, sine_grads(): jnp.dot(previous, hidden_weight[layer_index - 1], preferred_element_type=...  28.7 us
    dot_general x4, matrix products, sine_grads(): jnp.dot(inputs_rounded[layer_index - 1].T, rounded_grads[layer_index], pr...  16.2 us
    dot_general x4, matrix products, sine_grads(): output_grad = jnp.dot(cotan_rows, last_act, precision=lax.Precision.HIGHEST)  15.8 us
    dot_general x4, matrix products, sine_grads(): jnp.dot(rounded_grads[layer_index], hidden_weight[layer_index - 1].T, pre...  15.3 us
    ppermute x4, starting transfers between devices, padded_2(): lax.ppermute(lax.slice_in_dim(block, 0, width, axis=dim), axis, backward)  10.2 us
  transfers between devices with their start and end apart: 12, of which 5 were waited for; matrix products, arithmetic and copies ran while one was open for 5% of the time, Pallas kernels for 0%

profile of v1, /device:TPU:0, one launch (start us, length us, event | category | flops | bytes accessed | tf_op | source)
XLA Modules:
  0.0 433.7 jit_solution(16693888376495259913)
XLA Ops:
  8.0 5.1 %collective-permute-start.1 = (bf16[1,16,256]{2,1,0:T(8,128)(2,1)S(1)}, bf16[1,16,256]{2,1,0:T(8,128)(2,1)S(1)}, u32[]{:S(2)}, u32[]{:S(2)}) collective-permute-start(bf16[1,16,256]{2,1,0:T(8,128)(2,1)S(1)} %get-tuple-element.528), channel_id=1, source_target_pairs={{8,0},{16,8},{24,16},{0,24},{9,1},{17,9},{25,17},{1,25},{10,2},{18... | collective-permute-start | bytes 24584 | tf_op jit(solution)/shard_map/ppermute | solution.py:21
  16.9 6.2 %all-to-all-start = ((s32[32,1,192]{2,1,0:T(1,128)}), s32[32,1,192]{2,1,0:T(1,128)}, u32[]{:S(2)}, u32[]{:S(2)}) async-start(s32[32,1,192]{2,1,0:T(1,128)} %reshape.659), calls=%async_computation | async-start | bytes 65536 | tf_op jit(solution)/shard_map/all_to_all | solution.py:256
  37.4 4.9 %all-to-all-start.1 = ((f32[32,1,64]{2,1,0:T(1,128)}), f32[32,1,64]{2,1,0:T(1,128)S(1)}, u32[]{:S(2)}, u32[]{:S(2)}) async-start(f32[32,1,64]{2,1,0:T(1,128)} %bitcast.22), calls=%async_computation.1 | async-start | bytes 32768 | tf_op jit(solution)/shard_map/all_to_all | solution.py:257
  44.4 5.0 %all-to-all-done.1 = f32[32,1,64]{2,1,0:T(1,128)S(1)} async-done(((f32[32,1,64]{2,1,0:T(1,128)}), f32[32,1,64]{2,1,0:T(1,128)S(1)}, u32[]{:S(2)}, u32[]{:S(2)}) %all-to-all-start.1) | async-done | bytes 8224 | tf_op jit(solution)/shard_map/all_to_all | solution.py:257
  49.4 109.4 %while.24 = (s32[]{:T(128)}, f32[256,1024]{1,0:T(8,128)S(1)}, f32[1024]{0:T(1024)S(1)}, f32[3,512]{1,0:T(4,128)S(1)}, f32[1,512,512]{2,1,0:T(8,128)}, /*index=5*...) while((s32[]{:T(128)}, f32[256,1024]{1,0:T(8,128)S(1)}, ...), condition=%wide.region_4.5_spmd.clone, body=%wide.region_2.4_spmd.clone.sunk | while | flops 1739577856 | bytes 41928784 | solution.py:206
  53.9 7.2 %fusion.204 = (bf16[512,512]{1,0:T(8,128)(2,1)S(1)}, f32[512,512]{1,0:T(8,128)S(1)}, f32[512,512]{1,0:T(8,128)S(1)}) fusion(f32[512]{0:T(512)S(1)} %copy-done.25, f32[512]{0:T(512)S(1)} %mul.582, f32[512,1024]{1,0:T(8,128)S(1)} %convolution_add_fusion.19, bf16[1,512,512]{2,1,0:T(8,128)(2,1)S(1)} %copy-done.24, f32[512]{0:T(512)S(1)} %bitcast.281, ...), kind=kOutput, calls=%fused_computation.233.clone.1 | convolution fusion | flops 271581184 | bytes 5259264 | tf_op jit(solution)/shard_map/while/body/eval_jaxpr/dot_general | solution.py:106
  61.1 4.0 fusion.208
  65.2 4.1 fusion.207
  81.3 7.2 %fusion.204 = (bf16[512,512]{1,0:T(8,128)(2,1)S(1)}, f32[512,512]{1,0:T(8,128)S(1)}, f32[512,512]{1,0:T(8,128)S(1)}) fusion(f32[512]{0:T(512)S(1)} %copy-done.25, f32[512]{0:T(512)S(1)} %mul.582, f32[512,1024]{1,0:T(8,128)S(1)} %convolution_add_fusion.19, bf16[1,512,512]{2,1,0:T(8,128)(2,1)S(1)} %copy-done.24, f32[512]{0:T(512)S(1)} %bitcast.281, ...), kind=kOutput, calls=%fused_computation.233.clone.1 | convolution fusion | flops 271581184 | bytes 5259264 | tf_op jit(solution)/shard_map/while/body/eval_jaxpr/dot_general | solution.py:106
  88.4 4.0 fusion.208
  92.5 4.1 fusion.207
  96.6 3.8 fusion.205
  108.5 7.2 %fusion.204 = (bf16[512,512]{1,0:T(8,128)(2,1)S(1)}, f32[512,512]{1,0:T(8,128)S(1)}, f32[512,512]{1,0:T(8,128)S(1)}) fusion(f32[512]{0:T(512)S(1)} %copy-done.25, f32[512]{0:T(512)S(1)} %mul.582, f32[512,1024]{1,0:T(8,128)S(1)} %convolution_add_fusion.19, bf16[1,512,512]{2,1,0:T(8,128)(2,1)S(1)} %copy-done.24, f32[512]{0:T(512)S(1)} %bitcast.281, ...), kind=kOutput, calls=%fused_computation.233.clone.1 | convolution fusion | flops 271581184 | bytes 5259264 | tf_op jit(solution)/shard_map/while/body/eval_jaxpr/dot_general | solution.py:106
  115.7 4.0 fusion.208
  119.8 4.1 fusion.207
  135.9 7.2 %fusion.204 = (bf16[512,512]{1,0:T(8,128)(2,1)S(1)}, f32[512,512]{1,0:T(8,128)S(1)}, f32[512,512]{1,0:T(8,128)S(1)}) fusion(f32[512]{0:T(512)S(1)} %copy-done.25, f32[512]{0:T(512)S(1)} %mul.582, f32[512,1024]{1,0:T(8,128)S(1)} %convolution_add_fusion.19, bf16[1,512,512]{2,1,0:T(8,128)(2,1)S(1)} %copy-done.24, f32[512]{0:T(512)S(1)} %bitcast.281, ...), kind=kOutput, calls=%fused_computation.233.clone.1 | convolution fusion | flops 271581184 | bytes 5259264 | tf_op jit(solution)/shard_map/while/body/eval_jaxpr/dot_general | solution.py:106
  143.0 4.0 fusion.208
  147.1 4.1 fusion.207
  158.8 5.0 %copy.33 = f32[4,8,128,256]{3,1,2,0:T(8,128)S(1)} copy(f32[4,8,128,256]{3,2,1,0:T(8,128)} %get-tuple-element.323) | data formatting | bytes 8388608
  173.8 80.2 %all-reduce.7.cloned.1.call-done = (f32[9,256,256]{2,1,0:T(8,128)}, f32[256,1024]{1,0:T(8,128)}, f32[1,512,512]{2,1,0:T(8,128)}) async-done(((f32[9,256,256]{2,1,0:T(8,128)}, f32[256,1024]{1,0:T(8,128)}, f32[1,512,512]{2,1,0:T(8,128)}), (f32[9,256,256]{2,1,0:T(8,128)}, f32[256,1024]{1,0:T(8,128)}, f32[1,512,512]{2,1,0:T(8,128)})) %all-reduce.7.cloned.1.call-update) | async-done | bytes 4456464 | tf_op jit(solution)/shard_map/psum | solution.py:294
  255.7 23.7 %all-reduce = (f32[1024]{0:T(1024)S(1)}, f32[3,512]{1,0:T(4,128)S(1)}, f32[512]{0:T(512)S(1)}) all-reduce(f32[1024]{0:T(1024)S(1)} %get-tuple-element.325, f32[3,512]{1,0:T(4,128)S(1)} %get-tuple-element.326, f32[512]{0:T(512)S(1)} %copy-done.22), channel_id=1, replica_groups=mesh['lat'=4,'lon'=8] {'lon'}, use_global_device_ids=true, to_apply=%region_9.10 | all-reduce | flops 3072 | bytes 24576 | tf_op jit(solution)/shard_map/psum | solution.py:294
  279.3 20.5 %all-reduce.2 = (f32[1024]{0:T(1024)S(1)}, f32[3,512]{1,0:T(4,128)S(1)}, f32[512]{0:T(512)S(1)}) all-reduce(f32[1024]{0:T(1024)S(1)} %get-tuple-element.465, f32[3,512]{1,0:T(4,128)S(1)} %get-tuple-element.466, f32[512]{0:T(512)S(1)} %get-tuple-element.467), channel_id=1, replica_groups=mesh['lat'=4,'lon'=8] {'lat'}, use_global_device_ids=true, to_apply=%region_10.11 | all-reduce | flops 3072 | bytes 24576 | tf_op jit(solution)/shard_map/psum | solution.py:294
  301.3 3.9 collective-permute-done.5
  312.3 108.6 %all-reduce.9.cloned.1.call-done = (f32[9,256,256]{2,1,0:T(8,128)}, f32[256,1024]{1,0:T(8,128)}, f32[1,512,512]{2,1,0:T(8,128)}) async-done(((f32[9,256,256]{2,1,0:T(8,128)}, f32[256,1024]{1,0:T(8,128)}, f32[1,512,512]{2,1,0:T(8,128)}), (f32[9,256,256]{2,1,0:T(8,128)}, f32[256,1024]{1,0:T(8,128)}, f32[1,512,512]{2,1,0:T(8,128)})) %all-reduce.9.cloned.1.call-update) | async-done | bytes 4456464 | tf_op jit(solution)/shard_map/psum | solution.py:294
  (334 shorter events, 90.7 us)
Async XLA Ops:
  7.2 24.5 %copy-start.2 = (bf16[9,256,256]{2,1,0:T(8,128)(2,1)S(1)}, bf16[9,256,256]{2,1,0:T(8,128)(2,1)}, u32[]{:S(2)}) copy-start(bf16[9,256,256]{2,1,0:T(8,128)(2,1)} %param.14) | copy-start | bytes 3538948
  8.0 17.2 %collective-permute-start.1 = (bf16[1,16,256]{2,1,0:T(8,128)(2,1)S(1)}, bf16[1,16,256]{2,1,0:T(8,128)(2,1)S(1)}, u32[]{:S(2)}, u32[]{:S(2)}) collective-permute-start(bf16[1,16,256]{2,1,0:T(8,128)(2,1)S(1)} %get-tuple-element.528), channel_id=1, source_target_pairs={{8,0},{16,8},{24,16},{0,24},{9,1},{17,9},{25,17},{1,25},{10,2},{18... | collective-permute-start | bytes 24584 | tf_op jit(solution)/shard_map/ppermute | solution.py:21
  13.1 11.2 %collective-permute-start = (bf16[1,16,256]{2,1,0:T(8,128)(2,1)S(1)}, bf16[1,16,256]{2,1,0:T(8,128)(2,1)S(1)}, u32[]{:S(2)}, u32[]{:S(2)}) collective-permute-start(bf16[1,16,256]{2,1,0:T(8,128)(2,1)S(1)} %get-tuple-element.529), channel_id=1, source_target_pairs={{0,8},{8,16},{16,24},{24,0},{1,9},{9,17},{17,25},{25,1},{2,10},{10... | collective-permute-start | bytes 24584 | tf_op jit(solution)/shard_map/ppermute | solution.py:18
  16.9 20.5 %all-to-all-start = ((s32[32,1,192]{2,1,0:T(1,128)}), s32[32,1,192]{2,1,0:T(1,128)}, u32[]{:S(2)}, u32[]{:S(2)}) async-start(s32[32,1,192]{2,1,0:T(1,128)} %reshape.659), calls=%async_computation | async-start | bytes 65536 | tf_op jit(solution)/shard_map/all_to_all | solution.py:256
  25.2 6.1 %collective-permute-start.2 = (bf16[18,1,256]{2,1,0:T(2,128)(2,1)S(1)}, bf16[18,1,256]{2,1,0:T(2,128)(2,1)S(1)}, u32[]{:S(2)}, u32[]{:S(2)}) collective-permute-start(bf16[18,1,256]{2,1,0:T(2,128)(2,1)S(1)} %get-tuple-element.524), channel_id=1, source_target_pairs={{0,1},{1,2},{2,3},{3,4},{4,5},{5,6},{6,7},{7,0},{8,9},{9,10},{10,1... | collective-permute-start | bytes 27656 | tf_op jit(solution)/shard_map/ppermute | solution.py:18
  25.5 5.8 %collective-permute-start.3 = (bf16[18,1,256]{2,1,0:T(2,128)(2,1)S(1)}, bf16[18,1,256]{2,1,0:T(2,128)(2,1)S(1)}, u32[]{:S(2)}, u32[]{:S(2)}) collective-permute-start(bf16[18,1,256]{2,1,0:T(2,128)(2,1)S(1)} %get-tuple-element.525), channel_id=1, source_target_pairs={{1,0},{2,1},{3,2},{4,3},{5,4},{6,5},{7,6},{0,7},{9,8},{10,9},{11,1... | collective-permute-start | bytes 27656 | tf_op jit(solution)/shard_map/ppermute | solution.py:21
  34.2 15.2 %copy-start.1 = (bf16[256,1024]{1,0:T(8,128)(2,1)S(1)}, bf16[256,1024]{1,0:T(8,128)(2,1)}, u32[]{:S(2)}) copy-start(bf16[256,1024]{1,0:T(8,128)(2,1)} %param.15) | copy-start | bytes 1572868
  34.2 15.2 %copy-start.19 = (f32[1024]{0:T(1024)S(1)}, f32[1024]{0:T(1024)}, u32[]{:S(2)}) copy-start(f32[1024]{0:T(1024)} %param.16) | copy-start | bytes 12292
  34.6 14.8 %copy-start.18 = (f32[3,512]{1,0:T(4,128)S(1)}, f32[3,512]{1,0:T(4,128)}, u32[]{:S(2)}) copy-start(f32[3,512]{1,0:T(4,128)} %param.17) | copy-start | bytes 18436
  37.4 12.1 %all-to-all-start.1 = ((f32[32,1,64]{2,1,0:T(1,128)}), f32[32,1,64]{2,1,0:T(1,128)S(1)}, u32[]{:S(2)}, u32[]{:S(2)}) async-start(f32[32,1,64]{2,1,0:T(1,128)} %bitcast.22), calls=%async_computation.1 | async-start | bytes 32768 | tf_op jit(solution)/shard_map/all_to_all | solution.py:257
  42.2 211.8 %all-reduce.7.cloned.1.call-start = ((), (), s32[]{:S(2)}) async-start(), calls=%async_computation.2 | async-start | bytes 8912896 | tf_op jit(solution)/shard_map/psum | solution.py:294
  53.9 11.2 %copy-start.20 = (f32[512]{0:T(512)S(1)}, f32[512]{0:T(512)}, u32[]{:S(2)}) copy-start(f32[512]{0:T(512)} %get-tuple-element.712) | copy-start | bytes 6148 | tf_op jit(solution)/shard_map/while
  53.9 11.2 %copy-start.4 = (f32[1,512,512]{2,1,0:T(8,128)S(1)}, f32[1,512,512]{2,1,0:T(8,128)}, u32[]{:S(2)}) copy-start(f32[1,512,512]{2,1,0:T(8,128)} %get-tuple-element.711) | copy-start | bytes 3145732 | tf_op jit(solution)/shard_map/while
  81.2 11.2 %copy-start.20 = (f32[512]{0:T(512)S(1)}, f32[512]{0:T(512)}, u32[]{:S(2)}) copy-start(f32[512]{0:T(512)} %get-tuple-element.712) | copy-start | bytes 6148 | tf_op jit(solution)/shard_map/while
  81.2 11.2 %copy-start.4 = (f32[1,512,512]{2,1,0:T(8,128)S(1)}, f32[1,512,512]{2,1,0:T(8,128)}, u32[]{:S(2)}) copy-start(f32[1,512,512]{2,1,0:T(8,128)} %get-tuple-element.711) | copy-start | bytes 3145732 | tf_op jit(solution)/shard_map/while
  108.5 11.2 %copy-start.20 = (f32[512]{0:T(512)S(1)}, f32[512]{0:T(512)}, u32[]{:S(2)}) copy-start(f32[512]{0:T(512)} %get-tuple-element.712) | copy-start | bytes 6148 | tf_op jit(solution)/shard_map/while
  108.5 11.2 %copy-start.4 = (f32[1,512,512]{2,1,0:T(8,128)S(1)}, f32[1,512,512]{2,1,0:T(8,128)}, u32[]{:S(2)}) copy-start(f32[1,512,512]{2,1,0:T(8,128)} %get-tuple-element.711) | copy-start | bytes 3145732 | tf_op jit(solution)/shard_map/while
  135.9 11.2 %copy-start.20 = (f32[512]{0:T(512)S(1)}, f32[512]{0:T(512)}, u32[]{:S(2)}) copy-start(f32[512]{0:T(512)} %get-tuple-element.712) | copy-start | bytes 6148 | tf_op jit(solution)/shard_map/while
  135.9 11.2 %copy-start.4 = (f32[1,512,512]{2,1,0:T(8,128)S(1)}, f32[1,512,512]{2,1,0:T(8,128)}, u32[]{:S(2)}) copy-start(f32[1,512,512]{2,1,0:T(8,128)} %get-tuple-element.711) | copy-start | bytes 3145732 | tf_op jit(solution)/shard_map/while
  173.7 247.2 %all-reduce.9.cloned.1.call-start = ((), (), s32[]{:S(2)}) async-start(), calls=%async_computation.3 | async-start | bytes 8912896 | tf_op jit(solution)/shard_map/psum | solution.py:294
  254.1 47.1 %collective-permute-start.4 = (bf16[1,16,256]{2,1,0:T(8,128)(2,1)S(1)}, bf16[1,16,256]{2,1,0:T(8,128)(2,1)S(1)}, u32[]{:S(2)}, u32[]{:S(2)}) collective-permute-start(bf16[1,16,256]{2,1,0:T(8,128)(2,1)S(1)} %get-tuple-element.527), channel_id=1, source_target_pairs={{0,8},{8,16},{16,24},{24,0},{1,9},{9,17},{17,25},{25,1},{2,10},{10... | collective-permute-start | bytes 24584 | tf_op jit(solution)/shard_map/ppermute | solution.py:18
  301.2 3.9 collective-permute-start.5
  305.2 4.1 collective-permute-start.6
  305.3 4.1 collective-permute-start.7
  (32 other events, 71.7 us)
Sparse Core Ops, SparseCore 0:
  173.8 80.1 all-reduce.6
  256.5 164.2 all-reduce.8
